TPU v7x, 256 devices: a whole 4x4x8 slice. The times are simulated.
256 devices in a mesh: grp: 8 (over z), ord: 32 (over x, y, core).
Axes of the slice: x: 4, y: 4, z: 8, core: 2. Of those that a mesh axis runs over, the one named last changes fastest.
Arguments:
- legendre: float32 [512, 1048576], P('ord', 'grp')
- lon_center: float32 [8], P('grp'), may hold values from 0 to 1
- counts: int32 [8, 32], P('grp'), may hold values from 1 to 4096, 98304 in all within a row
- column_index: int32 [3, 512], replicated, may hold values from 0 to 120, as said below
Outputs:
- factor: float32 [512, 512], replicated
Inputs may be any that keep to these rules, and one draw needn't show every extreme that they name: `column_index`: each column names a different coefficient: row 0 is its degree (at most 120), row 1 its order (at most the degree), row 2 is 1 for a sine term and 0 for a cosine term, and 0 at order 0. Each group's counts add up to 98304.
All inputs are finite; a program needn't handle non-finite values.
Results may differ from a plain program's by a relative error of at most 0.0003.
Values sent between devices are 32-bit elements; how exact they have to be, the bound alone decides.
A program may use at most 64 MiB of HBM per device.

v0:
```python
import math
import jax
import jax.numpy as jnp
from jax import lax
from jax.sharding import PartitionSpec as P

NMAX = 120
quarter_turn = math.pi / 2
track_span = 0.3
kaula_gain = 1.2
highest = lax.Precision.HIGHEST


def upper_factor(matrix):
    return jnp.linalg.cholesky(matrix).T


def block_grams(exchanged):
    blocks = exchanged[:, 0]
    return jnp.einsum("jkb,lkb->kjl", blocks, blocks, precision=highest)


def body(legendre, lon_center, counts, column_index):
    ord_size = lax.axis_size("ord")
    grp_size = lax.axis_size("grp")
    cols_dev, rows_grp = legendre.shape
    rows_dev = rows_grp // ord_size
    scaling = 1.0 / math.sqrt(rows_grp * grp_size)
    own_columns = lax.dynamic_slice_in_dim(
        column_index, lax.axis_index("ord") * cols_dev, cols_dev, 1
    )
    harmonic = own_columns[1].astype(jnp.float32)
    sine_part = own_columns[2].astype(jnp.float32)
    longitude = lon_center[0] + jnp.arange(rows_grp, dtype=jnp.float32) * (track_span / rows_grp)
    harmonic_wave = jnp.cos(
        harmonic[:, None] * longitude[None, :] - sine_part[:, None] * quarter_turn
    )
    slot_index = jnp.arange(rows_dev, dtype=jnp.int32)
    row_valid = (slot_index[None, :] < counts[0][:, None]).astype(jnp.float32).reshape(rows_grp)
    design = legendre * harmonic_wave * (row_valid * scaling)[None, :]
    block_rows = min(512, rows_dev)
    shaped = design.reshape(cols_dev, ord_size, rows_dev // block_rows, block_rows)
    block_gram = block_grams(lax.all_to_all(shaped, "ord", split_axis=1, concat_axis=0, tiled=True))
    local_gram = jnp.sum(block_gram, axis=0)
    degree = column_index[0].astype(jnp.float32)
    kaula_weight = kaula_gain * (degree / NMAX) ** 2
    regular = jnp.diag(kaula_weight * kaula_weight)
    normal = lax.psum(local_gram, ("grp", "ord")) + regular
    return upper_factor(normal)


def solution(mesh):
    placed = (P("ord", "grp"), P("grp"), P("grp", None), P())
    return jax.shard_map(body, mesh=mesh, in_specs=placed, out_specs=P(), check_vma=False)
```

profile of v0, /device:TPU:2, one launch (start us, length us, event | category | flops | bytes accessed | tf_op | source)
XLA Modules:
  0.0 538.6 jit_solution(2535784197587066006)
XLA Ops:
  6.5 0.8 constant_dynamic-slice_fusion
  7.3 0.8 select_bitcast_fusion.1
  8.8 0.2 multiply_add_fusion
  9.0 29.6 %multiply_multiply_fusion = f32[16,131072]{1,0:T(8,128)S(1)} fusion(f32[16,131072]{1,0:T(8,128)} %param.4, f32[131072]{0:T(1024)S(1)} %bitcast.48, f32[16]{0:T(128)S(1)} %multiply_bitcast_fusion, f32[131072]{0:T(1024)S(1)} %multiply_add_fusion, f32[16]{0:T(128)S(1)} %convert_bitcast_fusion), kind=kLoop, calls=%fused_computation | loop fusion | flops 8388608 | bytes 17825920 | tf_op jit(solution)/shard_map/mul | solution.py:40
  38.6 4.9 copy.41
  43.5 20.4 %copy.25 = f32[16,32,8,512]{3,0,2,1:T(8,128)S(1)} copy(f32[16,32,8,512]{3,2,1,0:T(8,128)S(1)} %bitcast.46) | data formatting | bytes 16777216 | tf_op jit(solution)/shard_map/reshape | solution.py:42
  63.8 100.5 %all_to_all.15 = f32[16,32,8,512]{3,0,2,1:T(8,128)S(1)} all-to-all(f32[16,32,8,512]{3,0,2,1:T(8,128)S(1)} %copy.25), channel_id=1, replica_groups=mesh['grp'=8,'ord'=32] {'ord'}, dimensions={1} | all-to-all | bytes 16777216 | tf_op jit(solution)/shard_map/all_to_all | solution.py:43
  164.3 1.9 copy.26
  166.2 16.1 %convolution_bitcast_fusion = f32[512,512]{0,1:T(8,128)} fusion(f32[512,8,512]{2,0,1:T(8,128)S(1)} %bitcast.44), kind=kOutput, calls=%fused_computation.1 | convolution fusion | flops 12884901888 | bytes 9437184 | tf_op jit(solution)/shard_map/jkb,lkb->kjl/dot_general | solution.py:20
  182.4 0.7 multiply_multiply_fusion.1
  183.1 259.9 %all-reduce.3.cloned.1.call-done = f32[512,512]{0,1:T(8,128)} async-done(((f32[512,512]{0,1:T(8,128)}), f32[512,512]{0,1:T(8,128)}) %all-reduce.3.cloned.1.call-update) | async-done | bytes 1048592 | tf_op jit(solution)/shard_map/psum | solution.py:48
  443.0 1.3 select_add_fusion
  444.3 0.3 copy.28
  444.7 1.4 fusion
  446.1 11.7 %cholesky.103 = f32[128,128]{1,0:T(8,128)S(1)} custom-call(f32[128,128]{1,0:T(8,128)S(1)} %cholesky.263), custom_call_target="Cholesky" | custom-call | tf_op jit(solution)/shard_map/jit(cholesky)/cholesky | solution.py:15
  457.9 9.8 %custom-call.27 = f32[1,128,128]{1,2,0:T(8,128)S(1)} custom-call(f32[1,128,128]{2,1,0:T(8,128)S(1)} %get-tuple-element.10), custom_call_target="InvertDiagBlocksLowerTriangular" | custom-call | tf_op jit(solution)/shard_map/jit(cholesky)/cholesky | solution.py:15
  467.7 0.3 fusion.3
  468.0 0.3 convolution_subtract_fusion
  468.4 11.7 %cholesky.215 = f32[128,128]{1,0:T(8,128)S(1)} custom-call(f32[128,128]{1,0:T(8,128)S(1)} %cholesky.267), custom_call_target="Cholesky" | custom-call | tf_op jit(solution)/shard_map/jit(cholesky)/cholesky | solution.py:15
  480.2 0.1 copy.30
  480.5 9.9 %custom-call.28 = f32[1,128,128]{1,2,0:T(8,128)S(1)} custom-call(f32[1,128,128]{2,1,0:T(8,128)S(1)} %get-tuple-element.8), custom_call_target="InvertDiagBlocksLowerTriangular" | custom-call | tf_op jit(solution)/shard_map/jit(cholesky)/cholesky | solution.py:15
  490.6 0.3 convolution_dynamic-update-slice_fusion
  490.9 0.6 convolution_subtract_fusion.1
  491.5 11.7 %cholesky.236 = f32[128,128]{1,0:T(8,128)S(1)} custom-call(f32[128,128]{1,0:T(8,128)S(1)} %cholesky.272), custom_call_target="Cholesky" | custom-call | tf_op jit(solution)/shard_map/jit(cholesky)/cholesky | solution.py:15
  503.4 9.8 %custom-call.29 = f32[1,128,128]{1,2,0:T(8,128)S(1)} custom-call(f32[1,128,128]{2,1,0:T(8,128)S(1)} %get-tuple-element.6), custom_call_target="InvertDiagBlocksLowerTriangular" | custom-call | tf_op jit(solution)/shard_map/jit(cholesky)/cholesky | solution.py:15
  513.2 0.3 convolution_dynamic-update-slice_fusion.1
  513.5 0.5 convolution_subtract_fusion.2
  514.0 11.7 %cholesky.253 = f32[128,128]{1,0:T(8,128)S(1)} custom-call(f32[128,128]{1,0:T(8,128)S(1)} %convolution_subtract_fusion.2), custom_call_target="Cholesky" | custom-call | tf_op jit(solution)/shard_map/jit(cholesky)/cholesky | solution.py:15
  525.8 0.7 compare_reduce_fusion.1
  526.5 0.6 compare_reduce_fusion
  527.2 0.7 compare_reduce_fusion.2
  530.4 1.1 select_bitcast_fusion
  (21 shorter events, 0.8 us)
Async XLA Ops:
  6.5 436.4 %all-reduce.3.cloned.1.call-start = ((), (), s32[]{:S(2)}) async-start(), calls=%async_computation.1 | async-start | bytes 2097152 | tf_op jit(solution)/shard_map/psum | solution.py:48
Sparse Core Ops, SparseCore 0:
  182.5 260.4 all-reduce.2
where the time goes:
time: 542 us; the launch traced here: 539 us
  waiting for transfers between devices  260 us (48%)
  other arithmetic  114 us (21%)
  blocking collectives  100 us (18%)
  local copies, waits for them, and re-layouts  29 us (5%)
  matrix products  18.5 us (3%)
  between operations  17 us (3%)
    psum x1, waiting for transfers between devices, body(): normal = lax.psum(local_gram, ('grp', 'ord')) + regular  260 us
    all_to_all x1, blocking collectives, body(): lax.all_to_all(shaped, 'ord', split_axis=1, concat_axis=0, tiled=True)  100 us
    another operation x14, other arithmetic, upper_factor(): return jnp.linalg.cholesky(matrix).T  78.6 us
    mul x1, other arithmetic, body(): design = legendre * harmonic_wave * (row_valid * scaling)[None, :]  29.6 us
    reshape x1, local copies, waits for them, and re-layouts, body(): design.reshape(cols_dev, ord_size, rows_dev // block_rows, block_rows)  20.4 us
    dot_general x1, matrix products, block_grams(): return jnp.einsum('jkb,lkb->kjl', blocks, blocks, precision=highest)  16.1 us
  transfers between devices with their start and end apart: 1, of which 1 were waited for; matrix products, arithmetic and copies ran while one was open for 0% of the time, Pallas kernels for 0%

commit v1 on v0

--- a/solution.py
+++ b/solution.py
@@ -9,6 +9,12 @@
 track_span = 0.3
 kaula_gain = 1.2
 highest = lax.Precision.HIGHEST
+
+
+def review_sizes(base_x, axis_key, mesh_name):
+    for to_i in (axis_key, mesh_name):
+        base_x = lax.psum(base_x, to_i)
+    return base_x
 
 
 def upper_factor(matrix):
@@ -45,7 +51,7 @@
     degree = column_index[0].astype(jnp.float32)
     kaula_weight = kaula_gain * (degree / NMAX) ** 2
     regular = jnp.diag(kaula_weight * kaula_weight)
-    normal = lax.psum(local_gram, ("grp", "ord")) + regular
+    normal = review_sizes(local_gram, "grp", "ord") + regular
     return upper_factor(normal)
 
 

time: 542 us -> 477 us (0.88)
  waiting for transfers between devices: 260 us -> 194 us
    psum x1 -> x2, waiting for transfers between devices: 260 us -> 194 us  [review_sizes(): base_x = lax.psum(base_x, to_i)]
  transfers between devices with their start and end apart: 1 -> 2, of which waited for: 1 -> 2; matrix products, arithmetic and copies ran while one was open for 0% -> 0% of each run, Pallas kernels for 0% -> 0%
where the time goes in v1:
time: 477 us; the launch traced here: 472 us
  waiting for transfers between devices  194 us (41%)
  other arithmetic  114 us (24%)
  blocking collectives  100 us (21%)
  local copies, waits for them, and re-layouts  29 us (6%)
  matrix products  18.4 us (4%)
  between operations  17 us (4%)
    psum x2, waiting for transfers between devices, review_sizes(): base_x = lax.psum(base_x, to_i)  194 us
    all_to_all x1, blocking collectives, body(): lax.all_to_all(shaped, 'ord', split_axis=1, concat_axis=0, tiled=True)  100 us
    another operation x14, other arithmetic, upper_factor(): return jnp.linalg.cholesky(matrix).T  78.6 us
    mul x1, other arithmetic, body(): design = legendre * harmonic_wave * (row_valid * scaling)[None, :]  29.6 us
    reshape x1, local copies, waits for them, and re-layouts, body(): design.reshape(cols_dev, ord_size, rows_dev // block_rows, block_rows)  20.4 us
    dot_general x1, matrix products, block_grams(): return jnp.einsum('jkb,lkb->kjl', blocks, blocks, precision=highest)  16.1 us
  transfers between devices with their start and end apart: 2, of which 2 were waited for; matrix products, arithmetic and copies ran while one was open for 0% of the time, Pallas kernels for 0%

profile of v1, /device:TPU:2, one launch (start us, length us, event | category | flops | bytes accessed | tf_op | source)
XLA Modules:
  0.0 472.3 jit_solution(758496039798460978)
XLA Ops:
  6.5 0.8 constant_dynamic-slice_fusion
  7.3 0.8 select_bitcast_fusion.1
  8.8 0.2 multiply_add_fusion
  9.0 29.6 %multiply_multiply_fusion = f32[16,131072]{1,0:T(8,128)S(1)} fusion(f32[16,131072]{1,0:T(8,128)} %param.4, f32[131072]{0:T(1024)S(1)} %bitcast.48, f32[16]{0:T(128)S(1)} %multiply_bitcast_fusion, f32[131072]{0:T(1024)S(1)} %multiply_add_fusion, f32[16]{0:T(128)S(1)} %convert_bitcast_fusion), kind=kLoop, calls=%fused_computation | loop fusion | flops 8388608 | bytes 17825920 | tf_op jit(solution)/shard_map/mul | solution.py:46
  38.6 4.9 %copy.41 = f32[2,8,256,512]{3,2,1,0:T(8,128)S(1)} copy(f32[2,8,256,512]{3,1,2,0:T(8,128)S(1)} %bitcast.45) | data formatting | bytes 16777216
  43.5 20.4 %copy.25 = f32[16,32,8,512]{3,0,2,1:T(8,128)S(1)} copy(f32[16,32,8,512]{3,2,1,0:T(8,128)S(1)} %bitcast.46) | data formatting | bytes 16777216 | tf_op jit(solution)/shard_map/reshape | solution.py:48
  63.9 100.5 %all_to_all.15 = f32[16,32,8,512]{3,0,2,1:T(8,128)S(1)} all-to-all(f32[16,32,8,512]{3,0,2,1:T(8,128)S(1)} %copy.25), channel_id=1, replica_groups=mesh['grp'=8,'ord'=32] {'ord'}, dimensions={1} | all-to-all | bytes 16777216 | tf_op jit(solution)/shard_map/all_to_all | solution.py:49
  164.3 1.9 copy.26
  166.3 16.1 %convolution_bitcast_fusion = f32[512,512]{0,1:T(8,128)} fusion(f32[512,8,512]{2,0,1:T(8,128)S(1)} %bitcast.44), kind=kOutput, calls=%fused_computation.1 | convolution fusion | flops 12884901888 | bytes 9437184 | tf_op jit(solution)/shard_map/jkb,lkb->kjl/dot_general | solution.py:26
  182.5 77.8 %all-reduce.4.cloned.1.call-done = f32[512,512]{0,1:T(8,128)} async-done(((f32[512,512]{0,1:T(8,128)}), f32[512,512]{0,1:T(8,128)}) %all-reduce.4.cloned.1.call-update) | async-done | bytes 1048592 | tf_op jit(solution)/shard_map/psum | solution.py:16
  260.3 0.7 multiply_multiply_fusion.1
  261.0 115.7 %all-reduce.6.cloned.1.call-done = f32[512,512]{0,1:T(8,128)} async-done(((f32[512,512]{0,1:T(8,128)}), f32[512,512]{0,1:T(8,128)}) %all-reduce.6.cloned.1.call-update) | async-done | bytes 1048592 | tf_op jit(solution)/shard_map/psum | solution.py:16
  376.8 1.3 select_add_fusion
  378.1 0.3 copy.28
  378.4 1.4 fusion
  379.9 11.7 %cholesky.103 = f32[128,128]{1,0:T(8,128)S(1)} custom-call(f32[128,128]{1,0:T(8,128)S(1)} %cholesky.263), custom_call_target="Cholesky" | custom-call | tf_op jit(solution)/shard_map/jit(cholesky)/cholesky | solution.py:21
  391.7 9.8 %custom-call.27 = f32[1,128,128]{1,2,0:T(8,128)S(1)} custom-call(f32[1,128,128]{2,1,0:T(8,128)S(1)} %get-tuple-element.10), custom_call_target="InvertDiagBlocksLowerTriangular" | custom-call | tf_op jit(solution)/shard_map/jit(cholesky)/cholesky | solution.py:21
  401.5 0.3 fusion.3
  401.8 0.3 convolution_subtract_fusion
  402.1 11.7 %cholesky.215 = f32[128,128]{1,0:T(8,128)S(1)} custom-call(f32[128,128]{1,0:T(8,128)S(1)} %cholesky.267), custom_call_target="Cholesky" | custom-call | tf_op jit(solution)/shard_map/jit(cholesky)/cholesky | solution.py:21
  414.2 10.0 %custom-call.28 = f32[1,128,128]{1,2,0:T(8,128)S(1)} custom-call(f32[1,128,128]{2,1,0:T(8,128)S(1)} %get-tuple-element.8), custom_call_target="InvertDiagBlocksLowerTriangular" | custom-call | tf_op jit(solution)/shard_map/jit(cholesky)/cholesky | solution.py:21
  424.4 0.3 convolution_dynamic-update-slice_fusion
  424.7 0.6 convolution_subtract_fusion.1
  425.3 11.7 %cholesky.236 = f32[128,128]{1,0:T(8,128)S(1)} custom-call(f32[128,128]{1,0:T(8,128)S(1)} %cholesky.272), custom_call_target="Cholesky" | custom-call | tf_op jit(solution)/shard_map/jit(cholesky)/cholesky | solution.py:21
  437.2 9.8 %custom-call.29 = f32[1,128,128]{1,2,0:T(8,128)S(1)} custom-call(f32[1,128,128]{2,1,0:T(8,128)S(1)} %get-tuple-element.6), custom_call_target="InvertDiagBlocksLowerTriangular" | custom-call | tf_op jit(solution)/shard_map/jit(cholesky)/cholesky | solution.py:21
  447.0 0.3 convolution_dynamic-update-slice_fusion.1
  447.3 0.5 convolution_subtract_fusion.2
  447.8 11.7 %cholesky.253 = f32[128,128]{1,0:T(8,128)S(1)} custom-call(f32[128,128]{1,0:T(8,128)S(1)} %convolution_subtract_fusion.2), custom_call_target="Cholesky" | custom-call | tf_op jit(solution)/shard_map/jit(cholesky)/cholesky | solution.py:21
  459.6 0.7 compare_reduce_fusion.1
  460.3 0.6 compare_reduce_fusion
  461.0 0.7 compare_reduce_fusion.2
  464.2 1.1 select_bitcast_fusion
  (24 shorter events, 1.0 us)
Async XLA Ops:
  6.5 253.7 %all-reduce.4.cloned.1.call-start = ((), (), s32[]{:S(2)}) async-start(), calls=%async_computation.1 | async-start | bytes 2097152 | tf_op jit(solution)/shard_map/psum | solution.py:16
  182.4 194.4 %all-reduce.6.cloned.1.call-start = ((), (), s32[]{:S(2)}) async-start(), calls=%async_computation.2 | async-start | bytes 2097152 | tf_op jit(solution)/shard_map/psum | solution.py:16
Sparse Core Ops, SparseCore 0:
  182.5 77.7 all-reduce.3
  263.5 113.2 all-reduce.5
